TPU v7x, 32 devices: a whole 2x2x4 slice. The times are simulated.
32 devices in a mesh: tile: 8 (over y, x, core), member: 4 (over z).
Axes of the slice: x: 2, y: 2, z: 4, core: 2. Of those that a mesh axis runs over, the one named last changes fastest.
Arguments:
- hx: bfloat16 [512, 32768], P('member', 'tile'), may hold values from -6 to 6
- obs_value: bfloat16 [32768], P('tile'), may hold values from -8 to 8
- obs_rinv: bfloat16 [32768], P('tile'), may hold values from 0.29882812 to 4
- obs_index: int32 [32, 1024], P('tile'), may hold values from 512 to 5631, as said below
- loc_weight: float32 [32, 1024], P(('tile', 'member')), may hold values from 0.05 to 1
- state: bfloat16 [512, 131072], P('member', 'tile'), may hold values from -6 to 6
Outputs:
- analysis: bfloat16 [512, 131072], P('member', 'tile')
Inputs may be any that keep to these rules, and one draw needn't show every extreme that they name: `obs_index`: row p lists 1024 distinct positions in the pool of tile p // 4: positions 0 .. 1023 are the last 1024 observations of the tile before it, the next 4096 the tile's own, the last 1024 the first observations of the tile after it; the tiles form a closed band. All positions of a row lie within 2048 consecutive positions.
All inputs are finite; a program needn't handle non-finite values.
Results may differ from a plain program's by a relative error of at most 0.012.
The roundings to bfloat16 on the way count: a program that leaves them out, or rounds other values in their place, can miss the bound.
Values may be sent and summed in bfloat16 or wider, within the bound.
No kernel may reach another device: no remote copies, remote signals or barrier semaphores. Data moves between devices by JAX's collectives and lax.ppermute only.
A program may use at most 64 MiB of HBM per device.

v0:
```python
import jax
import jax.numpy as jnp
from jax import lax
from jax.sharding import PartitionSpec as P

LOC = 1024
NS_ITERS = 3


def with_halo(block, sides, width):
    for axis, dim in sides:
        count = lax.axis_size(axis)
        forward = [(i, i + 1) for i in range(count - 1)]
        forward.append((count - 1, 0))
        backward = [(target, source) for source, target in forward]
        low = lax.ppermute(
            lax.slice_in_dim(block, block.shape[dim] - width, None, axis=dim), axis, forward
        )
        high = lax.ppermute(lax.slice_in_dim(block, 0, width, axis=dim), axis, backward)
        block = jnp.concatenate([low, block, high], axis=dim)
    return block


def product_f32(left, right, dims):
    return lax.dot_general(
        left.astype(jnp.float32),
        right.astype(jnp.float32),
        (dims, ((), ())),
        precision=lax.Precision.HIGHEST,
        preferred_element_type=jnp.float32,
    )


def analysis(obs_block, obs_pair, loc_row):
    members = obs_block.shape[0]
    block_f = obs_block.astype(jnp.float32)
    obs_mean = jnp.mean(block_f, axis=0)
    obs_root = jnp.sqrt(obs_pair[1].astype(jnp.float32) * loc_row)
    scaled = ((block_f - obs_mean) * obs_root).astype(jnp.bfloat16)
    innovation = (obs_pair[0].astype(jnp.float32) - obs_mean) * obs_root
    gram_matrix = product_f32(scaled, scaled, ((1,), (1,)))
    identity = jnp.eye(members, dtype=jnp.float32)
    system = gram_matrix + (members - 1.0) * identity
    projection = jnp.dot(scaled.astype(jnp.float32), innovation, precision=lax.Precision.HIGHEST)
    norm_a = jnp.sqrt(jnp.sum(system * system))
    upper_iter = system / norm_a
    lower_iter = identity
    for sweep in range(NS_ITERS):
        upper_b = upper_iter.astype(jnp.bfloat16)
        lower_b = lower_iter.astype(jnp.bfloat16)
        product = product_f32(lower_b, upper_b, ((1,), (0,)))
        half_step = (1.5 * identity - 0.5 * product).astype(jnp.bfloat16)
        if sweep + 1 < NS_ITERS:
            upper_iter = product_f32(upper_b, half_step, ((1,), (0,)))
        lower_iter = product_f32(half_step, lower_b, ((1,), (0,)))
    invroot = lower_iter / jnp.sqrt(norm_a)
    inner_w = jnp.dot(invroot, projection, precision=lax.Precision.HIGHEST)
    mean_w = jnp.dot(invroot, inner_w, precision=lax.Precision.HIGHEST)
    transform = jnp.sqrt(members - 1.0) * invroot + mean_w[:, None]
    return transform.astype(jnp.bfloat16)


def transform_state(transform, state_block):
    block_f = state_block.astype(jnp.float32)
    state_mean = jnp.mean(block_f, axis=0)
    state_pert = (block_f - state_mean).astype(jnp.bfloat16)
    combined = product_f32(transform, state_pert, ((0,), (0,)))
    return (state_mean + combined).astype(jnp.bfloat16)


def on_device(hx, obs_value, obs_rinv, obs_index, loc_weight, state):
    ens_dev = hx.shape[0]
    member_pos = lax.axis_index("member")
    stacked = jnp.concatenate([hx, obs_value[None, :], obs_rinv[None, :]], axis=0)
    obs_pool = with_halo(stacked, (("tile", 1),), LOC)
    own_index = lax.dynamic_index_in_dim(obs_index, member_pos, 0, keepdims=False)
    obs_pair = jnp.take(obs_pool[ens_dev:], own_index, axis=1)
    picked = jnp.take(obs_pool[:ens_dev], obs_index, axis=1)
    received = lax.all_to_all(picked, "member", split_axis=1, concat_axis=0, tiled=True)
    obs_block = received[:, 0, :]
    transform = analysis(obs_block, obs_pair, loc_weight[0])
    group_count = obs_index.shape[0]
    state_split = state.reshape(ens_dev, group_count, state.shape[1] // group_count)
    updated = transform_state(
        transform,
        lax.all_to_all(state_split, "member", split_axis=1, concat_axis=0, tiled=True)[:, 0, :],
    )
    result = lax.all_to_all(updated[:, None, :], "member", split_axis=0, concat_axis=1, tiled=True)
    return result.reshape(ens_dev, state.shape[1])


def solution(mesh):
    in_specs = (
        P("member", "tile"),
        P("tile"),
        P("tile"),
        P("tile", None),
        P(("tile", "member"), None),
        P("member", "tile"),
    )
    out_specs = P("member", "tile")
    return jax.shard_map(
        on_device, mesh=mesh, in_specs=in_specs, out_specs=out_specs, check_vma=False
    )
```

profile of v0, /device:TPU:0, one launch (start us, length us, event | category | flops | bytes accessed | tf_op | source)
XLA Modules:
  0.0 328.8 jit_solution(2803960686868438312)
XLA Ops:
  0.0 1.6 copy.52
  1.6 1.3 broadcast_in_dim.44
  2.9 1.3 broadcast_in_dim.45
  4.2 0.3 pad_maximum_fusion.3
  4.6 0.5 collective-permute-start
  5.1 2.9 collective-permute-start.1
  8.1 0.0 copy-done.1
  8.1 9.8 %collective-permute-done = bf16[130,1024]{0,1:T(8,128)(2,1)S(1)} collective-permute-done((bf16[130,1024]{0,1:T(8,128)(2,1)S(1)}, bf16[130,1024]{0,1:T(8,128)(2,1)S(1)}, u32[]{:S(2)}, u32[]{:S(2)}) %collective-permute-start) | collective-permute-done | bytes 266272 | tf_op jit(solution)/shard_map/ppermute | solution.py:16
  17.9 1.5 collective-permute-done.1
  19.3 10.2 %pad_maximum_fusion = bf16[130,6144]{0,1:T(8,128)(2,1)S(1)} fusion(bf16[130,1024]{0,1:T(8,128)(2,1)S(1)} %collective-permute-done.1, bf16[1,4096]{0,1:T(8,128)(2,1)S(1)} %broadcast_in_dim.45, bf16[1,4096]{0,1:T(8,128)(2,1)S(1)} %broadcast_in_dim.44, bf16[128,4096]{0,1:T(8,128)(2,1)S(1)} %copy.52, bf16[130,1024]{0,1:T(8,128)(2,1)S(1)} %collective-permute-done), kind=kLoop, calls=%fused_computation.7 | loop fusion | flops 7987200 | bytes 3194880 | tf_op jit(solution)/shard_map/concatenate | solution.py:20
  29.5 0.0 copy-start
  29.5 1.7 copy-done
  31.2 0.1 slice.28
  31.3 12.1 %gather_fusion = bf16[4096,128]{1,0:T(8,128)(2,1)S(1)} fusion(bf16[128,6144]{0,1:T(8,128)(2,1)S(1)} %slice.28, s32[4096]{0:T(1024)S(1)} %bitcast_clamp_fusion), kind=kCustom, calls=%fused_computation | custom fusion | bytes 2113536 | tf_op jit(solution)/shard_map/jit(_take)/gather | solution.py:78
  43.5 0.5 copy.55
  44.0 1.1 select_bitcast_fusion
  45.1 4.9 %all-to-all-start.1 = ((bf16[128,4,1024]{2,0,1:T(8,128)(2,1)}), bf16[128,4,1024]{2,0,1:T(8,128)(2,1)S(1)}, u32[]{:S(2)}, u32[]{:S(2)}) async-start(bf16[128,4,1024]{2,0,1:T(8,128)(2,1)} %select_bitcast_fusion), calls=%async_computation.1 | async-start | bytes 2097152 | tf_op jit(solution)/shard_map/all_to_all | solution.py:79
  50.0 4.7 %copy.65 = bf16[16,4,8,4096]{3,2,0,1:T(8,128)(2,1)} copy(bf16[16,4,8,4096]{3,2,1,0:T(8,128)(2,1)} %bitcast.79) | data formatting | bytes 8388608 | tf_op jit(solution)/shard_map/reshape | solution.py:83
  54.7 22.0 %all-to-all-done.1 = bf16[128,4,1024]{2,0,1:T(8,128)(2,1)S(1)} async-done(((bf16[128,4,1024]{2,0,1:T(8,128)(2,1)}), bf16[128,4,1024]{2,0,1:T(8,128)(2,1)S(1)}, u32[]{:S(2)}, u32[]{:S(2)}) %all-to-all-start.1) | async-done | bytes 1048608 | tf_op jit(solution)/shard_map/all_to_all | solution.py:79
  76.7 5.2 %all-to-all-start = ((bf16[128,4,4096]{2,0,1:T(8,128)(2,1)}), bf16[128,4,4096]{2,0,1:T(8,128)(2,1)}, u32[]{:S(2)}, u32[]{:S(2)}) async-start(bf16[128,4,4096]{2,0,1:T(8,128)(2,1)} %bitcast.76), calls=%async_computation | async-start | bytes 8388608 | tf_op jit(solution)/shard_map/all_to_all | solution.py:86
  81.9 3.2 gather_fusion.1
  85.1 0.1 copy.56
  85.3 0.2 convert_reduce_fusion
  85.5 0.3 fusion.4
  85.8 1.5 multiply_reduce_fusion
  88.0 0.4 fusion.5
  88.4 0.4 convolution_convert_fusion.3
  88.8 0.9 convolution_bitcast_fusion.1
  89.7 0.4 convolution_convert_fusion.2
  90.2 0.4 fusion.6
  90.6 0.4 convolution_convert_fusion.1
  91.1 0.4 convolution_convert_fusion
  91.5 0.4 fusion.7
  92.0 0.4 convolution_divide_fusion
  92.4 1.0 convolution_bitcast_fusion
  93.4 1.0 fusion.19
  94.4 81.2 %all-to-all-done = bf16[128,4,4096]{2,0,1:T(8,128)(2,1)} async-done(((bf16[128,4,4096]{2,0,1:T(8,128)(2,1)}), bf16[128,4,4096]{2,0,1:T(8,128)(2,1)}, u32[]{:S(2)}, u32[]{:S(2)}) %all-to-all-start) | async-done | bytes 4194336 | tf_op jit(solution)/shard_map/all_to_all | solution.py:86
  175.6 3.2 convert_reduce_fusion.1
  178.8 3.1 fusion
  181.8 4.6 %fusion.1 = bf16[512,1,4096]{2,0,1:T(8,128)(2,1)} fusion(bf16[512,4096]{1,0:T(8,128)(2,1)S(1)} %fusion, f32[4096]{0:T(1024)S(1)} %broadcast_multiply_fusion, f32[512,512]{1,0:T(8,128)S(1)} %convolution_divide_fusion, f32[512]{0:T(512)S(1)} %bitcast.82), kind=kOutput, calls=%fused_computation.5 | convolution fusion | flops 2152464384 | bytes 9455616 | tf_op jit(solution)/shard_map/dot_general | solution.py:25
  186.4 0.5 broadcast.126
  186.9 6.6 %reduce.6 = bf16[512,4096]{1,0:T(8,128)(2,1)} reduce(bf16[512,1,4096]{2,0,1:T(8,128)(2,1)} %fusion.1, bf16[]{:T(256)} %broadcast.126), dimensions={1}, to_apply=%copy.57.reduce_sub_computation | reduce | bytes 8388610 | tf_op jit(solution)/shard_map/broadcast_in_dim | solution.py:88
  193.5 6.2 %reshape.136 = bf16[4,2,262144]{2,1,0:T(2,128)(2,1)} reshape(bf16[512,4096]{1,0:T(8,128)(2,1)} %reduce.6) | data formatting | bytes 8388608
  199.7 98.7 %all_to_all.33 = bf16[4,2,262144]{2,1,0:T(2,128)(2,1)} all-to-all(bf16[4,2,262144]{2,1,0:T(2,128)(2,1)} %reshape.136), channel_id=1, replica_groups=mesh['tile'=8,'member'=4] {'member'}, dimensions={0} | all-to-all | bytes 8388608 | tf_op jit(solution)/shard_map/all_to_all | solution.py:88
  298.5 7.4 %reshape.137 = bf16[512,1,4096]{2,1,0:T(2,128)(2,1)} reshape(bf16[4,2,262144]{2,1,0:T(2,128)(2,1)} %all_to_all.33) | data formatting | bytes 8388608
  305.9 10.1 %copy.60 = bf16[512,1,4096]{2,0,1:T(8,128)(2,1)} copy(bf16[512,1,4096]{2,1,0:T(2,128)(2,1)} %reshape.137) | data formatting | bytes 8388608
  316.1 6.3 %copy.58 = bf16[128,4,1,4096]{0,3,1,2:T(8,128)(2,1)} copy(bf16[128,4,1,4096]{3,0,1,2:T(8,128)(2,1)} %bitcast.75) | data formatting | bytes 8388608 | tf_op jit(solution)/shard_map/all_to_all | solution.py:88
  322.4 6.4 %copy.59 = bf16[128,16384]{1,0:T(8,128)(2,1)} copy(bf16[128,16384]{0,1:T(8,128)(2,1)} %bitcast.77) | data formatting | bytes 8388608 | tf_op jit(solution)/shard_map/reshape | solution.py:89
  (15 shorter events, 0.1 us)
Async XLA Ops:
  0.0 8.1 %copy-start.1 = (s32[4,1024]{1,0:T(4,128)S(1)}, s32[4,1024]{1,0:T(4,128)}, u32[]{:S(2)}) copy-start(s32[4,1024]{1,0:T(4,128)} %param.9) | copy-start | bytes 49156
  4.6 13.3 %collective-permute-start = (bf16[130,1024]{0,1:T(8,128)(2,1)S(1)}, bf16[130,1024]{0,1:T(8,128)(2,1)S(1)}, u32[]{:S(2)}, u32[]{:S(2)}) collective-permute-start(bf16[130,1024]{0,1:T(8,128)(2,1)S(1)} %get-tuple-element.7), channel_id=1, source_target_pairs={{0,4},{4,8},{8,12},{12,16},{16,20},{20,24},{24,28},{28,0},{1,5},{5... | collective-permute-start | bytes 798728 | tf_op jit(solution)/shard_map/ppermute | solution.py:16
  5.1 14.2 %collective-permute-start.1 = (bf16[130,1024]{0,1:T(8,128)(2,1)S(1)}, bf16[130,1024]{0,1:T(8,128)(2,1)S(1)}, u32[]{:S(2)}, u32[]{:S(2)}) collective-permute-start(bf16[130,1024]{0,1:T(8,128)(2,1)S(1)} %get-tuple-element.8), channel_id=1, source_target_pairs={{4,0},{8,4},{12,8},{16,12},{20,16},{24,20},{28,24},{0,28},{5,1},{9... | collective-permute-start | bytes 798728 | tf_op jit(solution)/shard_map/ppermute | solution.py:19
  29.5 1.7 copy-start
  45.1 31.6 %all-to-all-start.1 = ((bf16[128,4,1024]{2,0,1:T(8,128)(2,1)}), bf16[128,4,1024]{2,0,1:T(8,128)(2,1)S(1)}, u32[]{:S(2)}, u32[]{:S(2)}) async-start(bf16[128,4,1024]{2,0,1:T(8,128)(2,1)} %select_bitcast_fusion), calls=%async_computation.1 | async-start | bytes 2097152 | tf_op jit(solution)/shard_map/all_to_all | solution.py:79
  76.7 5.2 %slice-start = ((bf16[130,6144]{0,1:T(8,128)(2,1)}), bf16[2,6144]{0,1:T(8,128)(2,1)S(1)}, s32[]{:S(2)}) async-start(bf16[130,6144]{0,1:T(8,128)(2,1)} %copy-done), calls=%async_computation.3 | async-start | bytes 3145728 | tf_op jit(solution)/shard_map/slice | solution.py:77
  76.7 8.6 %copy-start.2 = (f32[1,1024]{1,0:T(1,128)S(1)}, f32[1,1024]{1,0:T(1,128)}, u32[]{:S(2)}) copy-start(f32[1,1024]{1,0:T(1,128)} %param.10) | copy-start | bytes 12292
  76.7 98.9 %all-to-all-start = ((bf16[128,4,4096]{2,0,1:T(8,128)(2,1)}), bf16[128,4,4096]{2,0,1:T(8,128)(2,1)}, u32[]{:S(2)}, u32[]{:S(2)}) async-start(bf16[128,4,4096]{2,0,1:T(8,128)(2,1)} %bitcast.76), calls=%async_computation | async-start | bytes 8388608 | tf_op jit(solution)/shard_map/all_to_all | solution.py:86
where the time goes:
time: 330 us; the launch traced here: 329 us
  waiting for transfers between devices  114 us (35%)
  blocking collectives  98.7 us (30%)
  local copies, waits for them, and re-layouts  63.7 us (19%)
  other arithmetic  25 us (8%)
  starting transfers between devices  13.6 us (4%)
  matrix products  12.4 us (4%)
    all_to_all x1, blocking collectives, on_device(): lax.all_to_all(updated[:, None, :], 'member', split_axis=0, concat_axis=1...  98.7 us
    all_to_all x1, waiting for transfers between devices, on_device(): lax.all_to_all(state_split, 'member', split_axis=1, concat_axis=0, tiled=...  81.2 us
    unnamed x10, local copies, waits for them, and re-layouts  27.1 us
    all_to_all x1, waiting for transfers between devices, on_device(): lax.all_to_all(picked, 'member', split_axis=1, concat_axis=0, tiled=True)  22 us
    gather x2, local copies, waits for them, and re-layouts, on_device(): picked = jnp.take(obs_pool[:ens_dev], obs_index, axis=1)  12.7 us
    concatenate x1, other arithmetic, with_halo(): block = jnp.concatenate([low, block, high], axis=dim)  10.2 us
    ppermute x1, waiting for transfers between devices, with_halo(): lax.ppermute(lax.slice_in_dim(block, block.shape[dim] - width, None, axis...  9.77 us
    dot_general x10, matrix products, product_f32(): lax.dot_general(left.astype(jnp.float32), right.astype(jnp.float32), (dim...  9.54 us
  transfers between devices with their start and end apart: 4, of which 4 were waited for; matrix products, arithmetic and copies ran while one was open for 5% of the time, Pallas kernels for 0%

commit v1 on v0

--- a/solution.py
+++ b/solution.py
@@ -76,7 +76,19 @@
     own_index = lax.dynamic_index_in_dim(obs_index, member_pos, 0, keepdims=False)
     obs_pair = jnp.take(obs_pool[ens_dev:], own_index, axis=1)
     picked = jnp.take(obs_pool[:ens_dev], obs_index, axis=1)
-    received = lax.all_to_all(picked, "member", split_axis=1, concat_axis=0, tiled=True)
+    ways, here = (lax.axis_size("member"), lax.axis_index("member"))
+    width_2 = picked.shape[1] // ways
+    lengths = list(picked.shape)
+    lengths[1] = width_2
+    height = lengths[0]
+    lengths[0] = height * ways
+    full = jnp.zeros(lengths, picked.dtype)
+    for mask in range(ways):
+        part = lax.dynamic_slice_in_dim(picked, (here ^ mask) * width_2, width_2, axis=1)
+        if mask:
+            part = lax.ppermute(part, "member", [(d, d ^ mask) for d in range(ways)])
+        full = lax.dynamic_update_slice_in_dim(full, part, (here ^ mask) * height, axis=0)
+    received = full
     obs_block = received[:, 0, :]
     transform = analysis(obs_block, obs_pair, loc_weight[0])
     group_count = obs_index.shape[0]

time: 330 us -> 297 us (0.900)
  waiting for transfers between devices: 114 us -> 84 us
    all_to_all x1, waiting for transfers between devices: 81.2 us -> 0.01 us  [on_device(): lax.all_to_all(state_split, 'member', split_axis=1, concat_axis=0, tiled=...]
    ppermute x0 -> x3, waiting for transfers between devices: none -> 80.5 us  [on_device(): part = lax.ppermute(part, 'member', [(d, d ^ mask) for d in range(ways)])]
    all_to_all x1 -> x0, waiting for transfers between devices: 22 us -> none  [on_device(): lax.all_to_all(picked, 'member', split_axis=1, concat_axis=0, tiled=True)]
    ppermute x1, waiting for transfers between devices: 9.77 us -> 2.01 us  [with_halo(): lax.ppermute(lax.slice_in_dim(block, block.shape[dim] - width, None, axis...]
    all_to_all x1 -> x0, starting transfers between devices: 4.92 us -> none  [on_device(): lax.all_to_all(picked, 'member', split_axis=1, concat_axis=0, tiled=True)]
    ppermute x0 -> x3, starting transfers between devices: none -> 4.45 us  [on_device(): part = lax.ppermute(part, 'member', [(d, d ^ mask) for d in range(ways)])]
    gather x2 -> x1, local copies, waits for them, and re-layouts: 12.7 us -> 12.1 us  [on_device(): picked = jnp.take(obs_pool[:ens_dev], obs_index, axis=1)]
  transfers between devices with their start and end apart: 4 -> 6, of which waited for: 4 -> 4; matrix products, arithmetic and copies ran while one was open for 5% -> 13% of each run, Pallas kernels for 0% -> 0%
where the time goes in v1:
time: 297 us; the launch traced here: 296 us
  blocking collectives  98.4 us (33%)
  waiting for transfers between devices  84 us (28%)
  local copies, waits for them, and re-layouts  62.3 us (21%)
  other arithmetic  23.6 us (8%)
  starting transfers between devices  13.6 us (5%)
  matrix products  12.9 us (4%)
    all_to_all x1, blocking collectives, on_device(): lax.all_to_all(updated[:, None, :], 'member', split_axis=0, concat_axis=1...  98.4 us
    ppermute x3, waiting for transfers between devices, on_device(): part = lax.ppermute(part, 'member', [(d, d ^ mask) for d in range(ways)])  80.5 us
    unnamed x10, local copies, waits for them, and re-layouts  25.4 us
    gather x1, local copies, waits for them, and re-layouts, on_device(): picked = jnp.take(obs_pool[:ens_dev], obs_index, axis=1)  12.1 us
    dot_general x10, matrix products, product_f32(): lax.dot_general(left.astype(jnp.float32), right.astype(jnp.float32), (dim...  10.2 us
    concatenate x1, other arithmetic, with_halo(): block = jnp.concatenate([low, block, high], axis=dim)  7.28 us
    broadcast_in_dim x1, other arithmetic, on_device(): updated[:, None, :]  6.89 us
    reshape x1, local copies, waits for them, and re-layouts, on_device(): return result.reshape(ens_dev, state.shape[1])  6.36 us
  transfers between devices with their start and end apart: 6, of which 4 were waited for; matrix products, arithmetic and copies ran while one was open for 13% of the time, Pallas kernels for 0%

profile of v1, /device:TPU:0, one launch (start us, length us, event | category | flops | bytes accessed | tf_op | source)
XLA Modules:
  0.0 295.7 jit_solution(2780281211339479976)
XLA Ops:
  0.0 1.6 copy.35
  1.6 1.4 broadcast_in_dim.45
  3.1 1.3 broadcast_in_dim.46
  4.4 1.3 pad_maximum_fusion.3
  5.7 0.5 collective-permute-start
  6.2 2.9 collective-permute-start.1
  9.1 2.3 copy.48
  11.4 5.8 %all-to-all-start = ((bf16[128,4,4096]{2,0,1:T(8,128)(2,1)}), bf16[128,4,4096]{2,0,1:T(8,128)(2,1)}, u32[]{:S(2)}, u32[]{:S(2)}) async-start(bf16[128,4,4096]{2,0,1:T(8,128)(2,1)} %bitcast.72), calls=%async_computation | async-start | bytes 8388608 | tf_op jit(solution)/shard_map/all_to_all | solution.py:98
  17.2 2.0 collective-permute-done
  19.3 1.5 collective-permute-done.1
  20.7 7.3 %pad_maximum_fusion = bf16[130,6144]{0,1:T(8,128)(2,1)S(1)} fusion(bf16[130,1024]{0,1:T(8,128)(2,1)} %collective-permute-done.1, bf16[1,4096]{0,1:T(8,128)(2,1)S(1)} %broadcast_in_dim.46, bf16[1,4096]{0,1:T(8,128)(2,1)S(1)} %broadcast_in_dim.45, bf16[128,4096]{0,1:T(8,128)(2,1)S(1)} %copy.35, bf16[130,1024]{0,1:T(8,128)(2,1)} %collective-permute-done), kind=kLoop, calls=%fused_computation.7 | loop fusion | flops 7987200 | bytes 3194880 | tf_op jit(solution)/shard_map/concatenate | solution.py:20
  28.2 3.2 %gather_fusion.1 = bf16[1024,2]{1,0:T(8,128)(2,1)S(1)} fusion(bf16[2,6144]{0,1:T(8,128)(2,1)S(1)} %slice.29, s32[1024]{0:T(1024)S(1)} %broadcast_clamp_fusion), kind=kCustom, calls=%fused_computation.1 | custom fusion | bytes 12288 | tf_op jit(solution)/shard_map/jit(_take)/gather | solution.py:77
  31.5 0.2 select_bitcast_fusion
  31.9 12.1 %gather_fusion = bf16[4096,128]{1,0:T(8,128)(2,1)S(1)} fusion(bf16[128,6144]{0,1:T(8,128)(2,1)S(1)} %slice.28, s32[4096]{0:T(1024)S(1)} %bitcast_clamp_fusion), kind=kCustom, calls=%fused_computation | custom fusion | bytes 2113536 | tf_op jit(solution)/shard_map/jit(_take)/gather | solution.py:78
  44.1 1.2 broadcast_select_fusion
  45.4 3.7 %collective-permute-start.4 = (bf16[128,1,1024]{0,2,1:T(8,128)(2,1)S(1)}, bf16[128,1,1024]{0,2,1:T(8,128)(2,1)S(1)}, u32[]{:S(2)}, u32[]{:S(2)}) collective-permute-start(bf16[128,1,1024]{0,2,1:T(8,128)(2,1)S(1)} %get-tuple-element.9), channel_id=1, source_target_pairs={{0,3},{1,2},{2,1},{3,0},{4,7},{5,6},{6,5},{7,4},{8,11},{9,10},{10,... | collective-permute-start | bytes 786440 | tf_op jit(solution)/shard_map/ppermute | solution.py:89
  49.1 0.7 collective-permute-start.2
  49.8 0.1 convert_reduce_fusion.2
  50.0 0.2 copy.39
  50.2 0.2 sqrt_reduce_fusion
  50.6 50.3 %collective-permute-done.2 = bf16[128,1,1024]{0,2,1:T(8,128)(2,1)} collective-permute-done((bf16[128,1,1024]{0,2,1:T(8,128)(2,1)S(1)}, bf16[128,1,1024]{0,2,1:T(8,128)(2,1)}, u32[]{:S(2)}, u32[]{:S(2)}) %collective-permute-start.2) | collective-permute-done | bytes 262176 | tf_op jit(solution)/shard_map/ppermute | solution.py:89
  101.0 1.0 bitcast_dynamic-update-slice_fusion.3
  102.0 30.2 %collective-permute-done.3 = bf16[128,1,1024]{0,2,1:T(8,128)(2,1)} collective-permute-done((bf16[128,1,1024]{0,2,1:T(8,128)(2,1)S(1)}, bf16[128,1,1024]{0,2,1:T(8,128)(2,1)}, u32[]{:S(2)}, u32[]{:S(2)}) %collective-permute-start.3) | collective-permute-done | bytes 262176 | tf_op jit(solution)/shard_map/ppermute | solution.py:89
  132.2 1.0 bitcast_dynamic-update-slice_fusion.2
  133.3 0.2 convert_reduce_fusion
  133.5 2.1 multiply_reduce_fusion
  136.3 0.4 fusion.4
  136.8 0.4 convolution_convert_fusion.3
  137.2 0.7 convolution_bitcast_fusion.1
  137.9 0.4 convolution_convert_fusion.2
  138.4 0.4 fusion.5
  138.8 0.4 convolution_convert_fusion.1
  139.3 0.4 convolution_convert_fusion
  139.7 0.4 fusion.6
  140.2 0.4 convolution_divide_fusion
  140.6 1.0 convolution_bitcast_fusion
  141.6 1.0 fusion.13
  142.6 3.2 %convert_reduce_fusion.1 = f32[4096]{0:T(1024)S(1)} fusion(bf16[128,4,4096]{2,0,1:T(8,128)(2,1)} %all-to-all-done), kind=kLoop, calls=%fused_computation.12 | loop fusion | flops 4190208 | bytes 4210688 | tf_op jit(solution)/shard_map/reduce_sum | solution.py:65
  145.8 3.1 %fusion = bf16[512,4096]{1,0:T(8,128)(2,1)S(1)} fusion(f32[4096]{0:T(1024)S(1)} %broadcast_multiply_fusion, bf16[128,4,4096]{2,0,1:T(8,128)(2,1)} %all-to-all-done), kind=kLoop, calls=%fused_computation.3 | loop fusion | flops 6291456 | bytes 8404992 | tf_op jit(solution)/shard_map/convert_element_type | solution.py:66
  148.9 4.6 %fusion.1 = bf16[512,1,4096]{2,0,1:T(8,128)(2,1)} fusion(bf16[512,4096]{1,0:T(8,128)(2,1)S(1)} %fusion, f32[4096]{0:T(1024)S(1)} %broadcast_multiply_fusion, f32[512,512]{1,0:T(8,128)S(1)} %convolution_divide_fusion, f32[512]{0:T(512)S(1)} %bitcast.76), kind=kOutput, calls=%fused_computation.5 | convolution fusion | flops 2152464384 | bytes 9455616 | tf_op jit(solution)/shard_map/dot_general | solution.py:25
  153.4 0.5 broadcast.83
  153.9 6.9 %reduce.7 = bf16[512,4096]{1,0:T(8,128)(2,1)} reduce(bf16[512,1,4096]{2,0,1:T(8,128)(2,1)} %fusion.1, bf16[]{:T(256)} %broadcast.83), dimensions={1}, to_apply=%copy.40.reduce_sub_computation | reduce | bytes 8388610 | tf_op jit(solution)/shard_map/broadcast_in_dim | solution.py:100
  160.8 6.2 %reshape.103 = bf16[4,2,262144]{2,1,0:T(2,128)(2,1)} reshape(bf16[512,4096]{1,0:T(8,128)(2,1)} %reduce.7) | data formatting | bytes 8388608
  167.0 98.4 %all_to_all.24 = bf16[4,2,262144]{2,1,0:T(2,128)(2,1)} all-to-all(bf16[4,2,262144]{2,1,0:T(2,128)(2,1)} %reshape.103), channel_id=1, replica_groups=mesh['tile'=8,'member'=4] {'member'}, dimensions={0} | all-to-all | bytes 8388608 | tf_op jit(solution)/shard_map/all_to_all | solution.py:100
  265.4 7.4 %reshape.104 = bf16[512,1,4096]{2,1,0:T(2,128)(2,1)} reshape(bf16[4,2,262144]{2,1,0:T(2,128)(2,1)} %all_to_all.24) | data formatting | bytes 8388608
  272.9 10.1 %copy.43 = bf16[512,1,4096]{2,0,1:T(8,128)(2,1)} copy(bf16[512,1,4096]{2,1,0:T(2,128)(2,1)} %reshape.104) | data formatting | bytes 8388608
  283.0 6.3 %copy.41 = bf16[128,4,1,4096]{0,3,1,2:T(8,128)(2,1)} copy(bf16[128,4,1,4096]{3,0,1,2:T(8,128)(2,1)} %bitcast.71) | data formatting | bytes 8388608 | tf_op jit(solution)/shard_map/all_to_all | solution.py:100
  289.3 6.4 %copy.42 = bf16[128,16384]{1,0:T(8,128)(2,1)} copy(bf16[128,16384]{0,1:T(8,128)(2,1)} %bitcast.73) | data formatting | bytes 8388608 | tf_op jit(solution)/shard_map/reshape | solution.py:101
  (26 shorter events, 0.8 us)
Async XLA Ops:
  1.6 7.4 %copy-start = (bf16[128,16384]{1,0:T(8,128)(2,1)S(1)}, bf16[128,16384]{1,0:T(8,128)(2,1)}, u32[]{:S(2)}) copy-start(bf16[128,16384]{1,0:T(8,128)(2,1)} %param.11) | copy-start | bytes 12582916
  5.7 13.6 %collective-permute-start = (bf16[130,1024]{0,1:T(8,128)(2,1)}, bf16[130,1024]{0,1:T(8,128)(2,1)}, u32[]{:S(2)}, u32[]{:S(2)}) collective-permute-start(bf16[130,1024]{0,1:T(8,128)(2,1)} %get-tuple-element.7), channel_id=1, source_target_pairs={{0,4},{4,8},{8,12},{12,16},{16,20},{20,24},{24,28},{28,0},{1,5},{5... | collective-permute-start | bytes 798728 | tf_op jit(solution)/shard_map/ppermute | solution.py:16
  6.2 14.5 %collective-permute-start.1 = (bf16[130,1024]{0,1:T(8,128)(2,1)}, bf16[130,1024]{0,1:T(8,128)(2,1)}, u32[]{:S(2)}, u32[]{:S(2)}) collective-permute-start(bf16[130,1024]{0,1:T(8,128)(2,1)} %get-tuple-element.8), channel_id=1, source_target_pairs={{4,0},{8,4},{12,8},{16,12},{20,16},{24,20},{28,24},{0,28},{5,1},{9... | collective-permute-start | bytes 798728 | tf_op jit(solution)/shard_map/ppermute | solution.py:19
  11.4 5.8 %copy-start.1 = (s32[4,1024]{1,0:T(4,128)S(1)}, s32[4,1024]{1,0:T(4,128)}, u32[]{:S(2)}) copy-start(s32[4,1024]{1,0:T(4,128)} %param.9) | copy-start | bytes 49156
  11.4 131.2 %all-to-all-start = ((bf16[128,4,4096]{2,0,1:T(8,128)(2,1)}), bf16[128,4,4096]{2,0,1:T(8,128)(2,1)}, u32[]{:S(2)}, u32[]{:S(2)}) async-start(bf16[128,4,4096]{2,0,1:T(8,128)(2,1)} %bitcast.72), calls=%async_computation | async-start | bytes 8388608 | tf_op jit(solution)/shard_map/all_to_all | solution.py:98
  31.9 18.1 %copy-start.2 = (f32[1,1024]{1,0:T(1,128)S(1)}, f32[1,1024]{1,0:T(1,128)}, u32[]{:S(2)}) copy-start(f32[1,1024]{1,0:T(1,128)} %param.10) | copy-start | bytes 12292
  45.4 87.8 %collective-permute-start.4 = (bf16[128,1,1024]{0,2,1:T(8,128)(2,1)S(1)}, bf16[128,1,1024]{0,2,1:T(8,128)(2,1)S(1)}, u32[]{:S(2)}, u32[]{:S(2)}) collective-permute-start(bf16[128,1,1024]{0,2,1:T(8,128)(2,1)S(1)} %get-tuple-element.9), channel_id=1, source_target_pairs={{0,3},{1,2},{2,1},{3,0},{4,7},{5,6},{6,5},{7,4},{8,11},{9,10},{10,... | collective-permute-start | bytes 786440 | tf_op jit(solution)/shard_map/ppermute | solution.py:89
  49.1 83.1 %collective-permute-start.3 = (bf16[128,1,1024]{0,2,1:T(8,128)(2,1)S(1)}, bf16[128,1,1024]{0,2,1:T(8,128)(2,1)}, u32[]{:S(2)}, u32[]{:S(2)}) collective-permute-start(bf16[128,1,1024]{0,2,1:T(8,128)(2,1)S(1)} %get-tuple-element.10), channel_id=1, source_target_pairs={{0,2},{1,3},{2,0},{3,1},{4,6},{5,7},{6,4},{7,5},{8,10},{9,11},{10,... | collective-permute-start | bytes 786440 | tf_op jit(solution)/shard_map/ppermute | solution.py:89
  49.1 51.8 %collective-permute-start.2 = (bf16[128,1,1024]{0,2,1:T(8,128)(2,1)S(1)}, bf16[128,1,1024]{0,2,1:T(8,128)(2,1)}, u32[]{:S(2)}, u32[]{:S(2)}) collective-permute-start(bf16[128,1,1024]{0,2,1:T(8,128)(2,1)S(1)} %get-tuple-element.11), channel_id=1, source_target_pairs={{0,1},{1,0},{2,3},{3,2},{4,5},{5,4},{6,7},{7,6},{8,9},{9,8},{10,11... | collective-permute-start | bytes 786440 | tf_op jit(solution)/shard_map/ppermute | solution.py:89
